TPU v7x, 768 devices: a whole 4x8x12 slice. The times are simulated.
768 devices in a mesh: occ: 6 (over z_lo, core), row: 8 (over y), col: 16 (over x, z_hi).
Axes of the slice: x: 4, y: 8, z: 12 (z_hi: 4, z_lo: 3; z = z_hi * 3 + z_lo), core: 2. Of those that a mesh axis runs over, the one named last changes fastest.
Arguments:
- bra_factor: bfloat16 [3072, 2, 4096], P(('occ', 'col'), None, 'row'), may hold values from -0.5 to 0.5
- ket_factor: bfloat16 [3072, 2, 4096], P(('occ', 'row'), None, 'col'), may hold values from -0.5 to 0.5
- occ_energy: float32 [2], replicated, may hold values from -2 to -0.5
- virt_energy: float32 [4096], replicated, may hold values from 0.2 to 3
Outputs:
- amplitudes: bfloat16 [2, 2, 4096, 4096], P(None, None, 'row', 'col')
- gamma: float32 [3072, 2, 4096], P(('occ', 'col'), None, 'row')
All inputs are finite; a program needn't handle non-finite values.
Results may differ from a plain program's by a relative error of at most 0.002.
Values may be sent and summed in bfloat16 or wider, within the bound.
A program may use at most 32 MiB of HBM per device.

v0:
```python
import jax
import jax.numpy as jnp
from jax import lax
from jax.sharding import PartitionSpec as P


def make_amplitudes(coulomb, occ_energy, virt_first, virt_second):
    denominator = (
        occ_energy[:, None, None, None]
        + occ_energy[None, :, None, None]
        - virt_first[None, None, :, None]
        - virt_second[None, None, None, :]
    )
    return ((2.0 * coulomb - jnp.transpose(coulomb, (1, 0, 2, 3))) / denominator).astype(
        jnp.bfloat16
    )


def on_device(bra_factor, ket_factor, occ_energy, virt_energy):
    a_width = bra_factor.shape[2]
    b_width = ket_factor.shape[2]
    ket_whole = lax.all_gather(ket_factor, "row", axis=0, tiled=True)
    row_index = lax.axis_index("row")
    col_index = lax.axis_index("col")
    virt_first = lax.dynamic_slice_in_dim(virt_energy, row_index * a_width, a_width, 0)
    virt_second = lax.dynamic_slice_in_dim(virt_energy, col_index * b_width, b_width, 0)
    partial_sum = jnp.einsum(
        "qia,qjb->ijab",
        lax.all_gather(bra_factor, "col", axis=0, tiled=True),
        ket_whole,
        preferred_element_type=jnp.float32,
    )
    coulomb = lax.psum(partial_sum, "occ")
    amplitudes = make_amplitudes(coulomb, occ_energy, virt_first, virt_second)
    gamma = lax.psum_scatter(
        jnp.einsum("ijab,qjb->qia", amplitudes, ket_whole, preferred_element_type=jnp.float32),
        "col",
        scatter_dimension=0,
        tiled=True,
    )
    return (amplitudes, gamma)


def solution(mesh):
    placed = (P(("occ", "col"), None, "row"), P(("occ", "row"), None, "col"), P(), P())
    return jax.shard_map(
        on_device,
        mesh=mesh,
        in_specs=placed,
        out_specs=(P(None, None, "row", "col"), P(("occ", "col"), None, "row")),
        check_vma=False,
    )
```

profile of v0, /device:TPU:1, one launch (start us, length us, event | category | flops | bytes accessed | tf_op | source)
XLA Modules:
  0.0 402.3 jit_solution(810299030366579271)
XLA Ops:
  7.2 0.0 all-gather.2.cloned.1.call-start
  7.2 1.5 copy.13
  8.7 0.0 all-gather.2.cloned.1.call-update
  8.7 0.0 all-reduce.4.cloned.1.call-start
  8.8 0.9 copy.12
  9.6 22.5 %all_gather.6 = bf16[512,2,256]{2,0,1:T(8,128)(2,1)S(1)} all-gather(bf16[64,2,256]{2,0,1:T(8,128)(2,1)S(1)} %copy.12), channel_id=1, replica_groups=mesh['occ'=6,'row'=8,'col'=16] {'row'}, dimensions={0}, use_global_device_ids=true | all-gather | bytes 589824 | tf_op jit(solution)/shard_map/all_gather | solution.py:22
  32.1 0.0 copy-start
  32.1 0.0 copy-start.2
  32.1 58.7 %all-gather.2.cloned.1.call-done = bf16[512,2,512]{2,0,1:T(8,128)(2,1)} async-done(((bf16[32,2,512]{2,0,1:T(8,128)(2,1)}), bf16[512,2,512]{2,0,1:T(8,128)(2,1)}) %all-gather.2.cloned.1.call-update) | async-done | bytes 1048592 | tf_op jit(solution)/shard_map/all_gather | solution.py:29
  90.9 3.3 convolution_bitcast_fusion.1
  94.2 0.0 all-reduce.4.cloned.1.call-update
  94.2 0.0 copy-done
  94.2 0.0 all-reduce.6.cloned.1.call-start
  94.3 0.8 dynamic_slice.6
  95.0 0.8 dynamic_slice.7
  95.8 0.0 copy-done.2
  95.8 0.1 broadcast_add_fusion
  95.9 0.1 broadcast_subtract_fusion
  95.9 76.1 %all-reduce.4.cloned.1.call-done = f32[2,2,512,256]{2,3,0,1:T(8,128)} async-done(((f32[2,2,512,256]{2,3,0,1:T(8,128)}), f32[2,2,512,256]{2,3,0,1:T(8,128)}) %all-reduce.4.cloned.1.call-update) | async-done | bytes 2097168 | tf_op jit(solution)/shard_map/psum | solution.py:33
  172.0 0.0 copy-start.1
  172.0 2.9 fusion.1
  174.9 0.0 copy-done.1
  174.9 0.8 convolution_bitcast_fusion
  175.7 2.4 copy.16
  178.2 0.0 all-reduce.6.cloned.1.call-update
  178.2 1.3 dynamic-slice
  180.1 1.3 copy.17
  181.4 212.8 %all-reduce.6.cloned.1.call-done = f32[512,2,512]{2,1,0:T(2,128)} async-done(((f32[512,2,512]{2,1,0:T(2,128)}), f32[512,2,512]{2,1,0:T(2,128)}) %all-reduce.6.cloned.1.call-update) | async-done | bytes 2097168
  394.2 1.6 constant_dynamic-slice_fusion
Async XLA Ops:
  7.2 83.7 %all-gather.2.cloned.1.call-start = ((), (), s32[]{:S(2)}) async-start(), calls=%async_computation | async-start | bytes 1114112 | tf_op jit(solution)/shard_map/all_gather | solution.py:29
  8.7 163.3 %all-reduce.4.cloned.1.call-start = ((), (), s32[]{:S(2)}) async-start(), calls=%async_computation.1 | async-start | bytes 4194304 | tf_op jit(solution)/shard_map/psum | solution.py:33
  32.1 62.1 %copy-start = (bf16[512,2,256]{2,0,1:T(8,128)(2,1)}, bf16[512,2,256]{2,0,1:T(8,128)(2,1)S(1)}, u32[]{:S(2)}) copy-start(bf16[512,2,256]{2,0,1:T(8,128)(2,1)S(1)} %all_gather.6) | copy-start | bytes 1572868
  32.1 63.6 %copy-start.2 = (f32[2]{0:T(128)S(1)}, f32[2]{0:T(128)}, u32[]{:S(2)}) copy-start(f32[2]{0:T(128)} %param.6) | copy-start | bytes 28
  94.2 300.0 %all-reduce.6.cloned.1.call-start = ((), (), s32[]{:S(2)}) async-start(), calls=%async_computation.2 | async-start | bytes 4194304
  172.0 2.9 copy-start.1
Sparse Core Ops, SparseCore 0:
  12.2 78.5 all-gather.1
  94.3 77.6 all-reduce.3
  178.3 215.8 all-reduce.5
where the time goes:
time: 410 us; the launch traced here: 402 us
  waiting for transfers between devices  348 us (85%)
  blocking collectives  22.5 us (5%)
  between operations  14.4 us (4%)
  local copies, waits for them, and re-layouts  10.5 us (3%)
    unnamed x4, waiting for transfers between devices  213 us
    psum x1, waiting for transfers between devices, on_device(): coulomb = lax.psum(partial_sum, 'occ')  76.1 us
    all_gather x1, waiting for transfers between devices, on_device(): lax.all_gather(bra_factor, 'col', axis=0, tiled=True)  58.7 us
    all_gather x1, blocking collectives, on_device(): ket_whole = lax.all_gather(ket_factor, 'row', axis=0, tiled=True)  22.5 us
  transfers between devices with their start and end apart: 3, of which 3 were waited for; matrix products, arithmetic and copies ran while one was open for 1% of the time, Pallas kernels for 0%

commit v1 on v0

v1 whole, which is shorter than its diff:
```python
import functools

import jax
import jax.numpy as jnp
from jax import lax
from jax.experimental import pallas as pl
from jax.experimental.pallas import tpu as pltpu
from jax.sharding import PartitionSpec as P

NZL, NC, NY, NX, NZH = 3, 2, 8, 4, 4
WIN = 192
STARTS = (0, 160, 320)
KEEP = 176
BF, F32 = jnp.bfloat16, jnp.float32
NT = (((1,), (1,)), ((), ()))
TN = (((0,), (0,)), ((), ()))


def rem(value, n):
    return lax.rem(value, n)


def kernel(
    occ_ref, bra_ref, ket_ref, virt_ref, amp_ref, gam_ref,
    bra_all, ket_all, part, other, amps, va_col,
    rx_send, rx_recv, rx_own, rz_send, rz_recv, rzb_send, rzb_recv,
    bz_s, bz_r, bx_s, bx_r, kz_s, kz_r, ky_s, ky_r, p_s, p_r,
    ag_s, ag_r, fw_s, fw_r, rx_s, rx_r, rz_s, rz_r,
):
    occ, y, col = lax.axis_index("occ"), lax.axis_index("row"), lax.axis_index("col")
    zl, core = occ // 2, rem(occ, 2)
    x, zh = col // 4, rem(col, 4)

    def device(dx=0, dy=0, dzh=0, dzl=0, dcore=0):
        zl2, core2 = rem(zl + dzl, NZL), rem(core + dcore, NC)
        y2, x2, zh2 = rem(y + dy, NY), rem(x + dx, NX), rem(zh + dzh, NZH)
        return (zl2 * 2 + core2, y2, x2 * 4 + zh2)

    def send(src, dst, s_sem, r_sem, **where):
        return pltpu.make_async_remote_copy(
            src_ref=src, dst_ref=dst, send_sem=s_sem, recv_sem=r_sem,
            device_id=device(**where), device_id_type=pl.DeviceIdType.MESH,
        )

    z_peers = [(e, d) for e in range(3) for d in range(4) if (e, d) != (0, 0)]
    peers = [dict(dzl=e, dzh=d) for e, d in z_peers]
    peers += [dict(dx=d) for d in (1, 2, 3)] + [dict(dy=1), dict(dy=NY - 1), dict(dcore=1)]
    barrier = pltpu.get_barrier_semaphore()
    for peer in peers:
        pl.semaphore_signal(barrier, inc=1, device_id=device(**peer), device_id_type=pl.DeviceIdType.MESH)
    pl.semaphore_wait(barrier, len(peers))

    pending = []

    def start(copy):
        copy.start()
        pending.append(copy)

    def bra_rows(zl_src, x_src, zh_src=0):
        return pl.multiple_of(zl_src * 512 + x_src * 128 + zh_src * 32, 32)

    def ket_rows(zl_src, y_src):
        return pl.multiple_of(zl_src * 512 + y_src * 64, 64)

    own_ket = ket_rows(zl, y)

    def ket_z(e):
        return send(ket_ref, ket_all.at[pl.ds(own_ket, 64)], kz_s.at[e], kz_r.at[e], dzl=e)

    def ket_y(e, way, step):
        zl_src = rem(zl + 3 - e, 3)
        hop = 1 if way == 0 else NY - 1
        y_src = rem(y + (NY - step + 1 if way == 0 else step - 1), NY)
        rows = ket_rows(zl_src, y_src)
        size = 64 if step < 4 else 32
        rows = pl.multiple_of(rows + (32 if step == 4 and way == 1 else 0), 32)
        here = ket_all.at[pl.ds(rows, size)]
        src = ket_ref if (step == 1 and e == 0) else here
        k = (e * 2 + way) * 4 + step - 1
        return send(src, here, ky_s.at[k], ky_r.at[k], dy=hop)

    def bra_z(e, d):
        there = bra_all.at[pl.ds(bra_rows(zl, x, zh), 32)]
        return send(bra_ref.at[rem(zl + e, 3)], there, bz_s.at[e * 4 + d], bz_r.at[e * 4 + d], dzl=e, dzh=d)

    def bra_x(e, dx):
        here = bra_all.at[pl.ds(bra_rows(rem(zl + 3 - e, 3), x), 128)]
        return send(here, here, bx_s.at[e * 3 + dx - 1], bx_r.at[e * 3 + dx - 1], dx=dx)

    for e in (1, 2):
        start(ket_z(e))
    for way in (0, 1):
        start(ket_y(0, way, 1))
    for e, d in [(0, 1), (0, 3), (0, 2)] + [(e, d) for e in (1, 2) for d in (0, 1, 3, 2)]:
        start(bra_z(e, d))
    ket_all[pl.ds(own_ket, 64), :] = ket_ref[...]
    bra_all[pl.ds(bra_rows(zl, x, zh), 32), :] = bra_ref[zl]

    for t in range(4):
        row = virt_ref[pl.ds(y * 4 + t, 1), :]
        va_col[pl.ds(t * 128, 128), :] = jnp.transpose(jnp.broadcast_to(row, (128, 128)))

    for e in (1, 2):
        ket_z(e).wait_recv()
        for way in (0, 1):
            start(ket_y(e, way, 1))

    for step in (2, 3, 4):
        e = step - 2
        for e2 in range(3):
            for way in (0, 1):
                ket_y(e2, way, step - 1).wait_recv()
                start(ket_y(e2, way, step))
        for d in range(4):
            if (e, d) != (0, 0):
                bra_z(e, d).wait_recv()
        for dx in (1, 2, 3):
            start(bra_x(e, dx))

    for e in range(3):
        for dx in (1, 2, 3):
            bra_x(e, dx).wait_recv()
        for way in (0, 1):
            ket_y(e, way, 4).wait_recv()
        rows = pl.ds(pl.multiple_of(rem(zl + 3 - e, 3) * 512, 512), 512)
        term = lax.dot_general(bra_all[rows, :], ket_all[rows, :], TN, preferred_element_type=F32)
        if e == 0:
            part[...] = term
        else:
            part[...] += term
    swap = send(part, other, p_s.at[0], p_r.at[0], dcore=1)
    start(swap)
    vb_rows = virt_ref[pl.ds(col * 2, 2), :]
    vb = jnp.concatenate([vb_rows[0:1], vb_rows[1:2]], axis=1)
    va = va_col[pl.ds(pl.multiple_of(zl * 160, 32), WIN), :]
    va = jnp.concatenate([va, va], axis=1)
    swap.wait_recv()

    def coulomb(i, j):
        rows, cols = pl.ds(i * WIN, WIN), pl.ds(j * 256, 256)
        return part[rows, cols] + other[rows, cols]

    for i in range(2):
        for j in range(2):
            den = ((occ_ref[i] + occ_ref[j]) - va) - vb
            amps[j, pl.ds(i * WIN, WIN), :] = ((2.0 * coulomb(i, j) - coulomb(j, i)) / den).astype(BF)
    skip = pl.multiple_of(jnp.where(zl == 2, WIN - KEEP, 0), 16)

    def amp_z(e):
        src = amps.at[:, pl.ds(pl.multiple_of(core * WIN + skip, 16), KEEP), :]
        return send(src, amp_ref.at[zl, core], ag_s.at[e], ag_r.at[e], dzl=e)

    def amp_core(e):
        here = amp_ref.at[rem(zl + 3 - e, 3), core]
        return send(here, here, fw_s.at[e], fw_r.at[e], dcore=1)

    def rx(e, dx):
        k = e * 3 + dx - 1
        return send(rx_send.at[k], rx_recv.at[k], rx_s.at[k], rx_r.at[k], dx=dx)

    def rz(e, d):
        k = e * 4 + d
        if d == 2:
            return send(rzb_send.at[e], rzb_recv.at[e], rz_s.at[k], rz_r.at[k], dzl=e, dzh=d)
        return send(rz_send.at[k], rz_recv.at[k], rz_s.at[k], rz_r.at[k], dzl=e, dzh=d)

    order = (1, 2, 0)
    for n, e in enumerate(order):
        for dx in (2, 1, 3, 0):
            rows = pl.ds(bra_rows(rem(zl + e, 3), rem(x + dx, 4)), 128)
            block = lax.dot_general(ket_all[rows, 0:256], amps[0], NT, preferred_element_type=F32)
            block += lax.dot_general(ket_all[rows, 256:512], amps[1], NT, preferred_element_type=F32)
            if dx == 0:
                rx_own[e] = block
            else:
                rx_send[e * 3 + dx - 1] = block.astype(BF)
                start(rx(e, dx))
        if n == 0:
            for e2 in (1, 2):
                start(amp_z(e2))
    for i in range(2):
        for j in range(2):
            amp_ref[zl, i, j] = amps[j, pl.ds(pl.multiple_of(i * WIN + skip, 16), KEEP), :]
    for e in order:
        for dx in (1, 2, 3):
            rx(e, dx).wait_recv()
        for d in (2, 1, 3, 0):
            rows = pl.ds(pl.multiple_of(rem(zh + d, 4) * 32, 32), 32)
            total = rx_own[e, rows, :]
            for dx in (1, 2, 3):
                total += rx_recv[e * 3 + dx - 1, rows, :].astype(F32)
            if d == 2:
                rzb_send[e] = total.astype(BF)
            else:
                rz_send[e * 4 + d] = total
            if (e, d) != (0, 0):
                start(rz(e, d))
    for e in (1, 2):
        amp_z(e).wait_recv()
        start(amp_core(e))
    for e in order:
        for d in range(4):
            if (e, d) != (0, 0):
                rz(e, d).wait_recv()
        first = rz_send[0] if e == 0 else rz_recv[e * 4]
        total = (first + rz_recv[e * 4 + 1]) + (rz_recv[e * 4 + 3] + rzb_recv[e].astype(F32))
        gam_ref[rem(zl + 3 - e, 3)] = total
    for e in (1, 2):
        amp_core(e).wait_recv()
    for copy in pending:
        copy.wait_send()


def on_device(bra_factor, ket_factor, occ_energy, virt_energy):
    windows = jnp.stack([bra_factor[:, :, s : s + WIN] for s in STARTS])
    dma = pltpu.SemaphoreType.DMA
    vmem = pl.BlockSpec(memory_space=pltpu.VMEM)
    amp, gam = pl.pallas_call(
        kernel,
        out_shape=(
            jax.ShapeDtypeStruct((3, 2, 2, KEEP, 256), BF),
            jax.ShapeDtypeStruct((3, 32, 2 * WIN), F32),
        ),
        in_specs=[pl.BlockSpec(memory_space=pltpu.SMEM), vmem, vmem, vmem],
        out_specs=(vmem, vmem),
        scratch_shapes=[
            pltpu.VMEM((1536, 2 * WIN), BF),
            pltpu.VMEM((1536, 512), BF),
            pltpu.VMEM((2 * WIN, 512), F32),
            pltpu.VMEM((2 * WIN, 512), F32),
            pltpu.VMEM((2, 2 * WIN, 256), BF),
            pltpu.VMEM((512, 128), F32),
            pltpu.VMEM((9, 128, 2 * WIN), BF),
            pltpu.VMEM((9, 128, 2 * WIN), BF),
            pltpu.VMEM((3, 128, 2 * WIN), F32),
            pltpu.VMEM((12, 32, 2 * WIN), F32),
            pltpu.VMEM((12, 32, 2 * WIN), F32),
            pltpu.VMEM((3, 32, 2 * WIN), BF),
            pltpu.VMEM((3, 32, 2 * WIN), BF),
            dma((12,)), dma((12,)), dma((9,)), dma((9,)), dma((3,)), dma((3,)),
            dma((24,)), dma((24,)), dma((1,)), dma((1,)),
            dma((3,)), dma((3,)), dma((3,)), dma((3,)), dma((9,)), dma((9,)), dma((12,)), dma((12,)),
        ],
        compiler_params=pltpu.CompilerParams(
            collective_id=0, has_side_effects=True, vmem_limit_bytes=48 << 20
        ),
    )(occ_energy, windows.reshape(3, 32, 2 * WIN), ket_factor.reshape(64, 512), virt_energy.reshape(32, 128))
    amplitudes = jnp.concatenate([amp[0], amp[1][:, :, 16:], amp[2]], axis=2)
    gam = gam.reshape(3, 32, 2, WIN)
    gamma = jnp.concatenate(
        [gam[0][:, :, :KEEP], gam[1][:, :, 16:KEEP], gam[2][:, :, 16:]], axis=2
    )
    return (amplitudes, gamma)


def solution(mesh):
    placed = (P(("occ", "col"), None, "row"), P(("occ", "row"), None, "col"), P(), P())
    return jax.shard_map(
        on_device,
        mesh=mesh,
        in_specs=placed,
        out_specs=(P(None, None, "row", "col"), P(("occ", "col"), None, "row")),
        check_vma=False,
    )
```

time: 410 us -> 84.7 us (0.21); the launches traced: 402 us -> 84.4 us
  waiting for transfers between devices: 348 us -> 0 us
  Pallas kernels: 0 us -> 77.6 us
  blocking collectives: 22.5 us -> 0 us
  between operations: 14.4 us -> 0.73 us
  local copies, waits for them, and re-layouts: 10.5 us -> 4.19 us
    unnamed x4 -> x0, waiting for transfers between devices: 213 us -> none
    pallas_call x0 -> x1, Pallas kernels: none -> 77.6 us  [on_device(): pl.pallas_call(kernel, out_shape=(jax.ShapeDtypeStruct((3, 2, 2, KEEP, 25...]
    psum x1 -> x0, waiting for transfers between devices: 76.1 us -> none  [on_device(): coulomb = lax.psum(partial_sum, 'occ')]
    all_gather x1 -> x0, waiting for transfers between devices: 58.7 us -> none  [on_device(): lax.all_gather(bra_factor, 'col', axis=0, tiled=True)]
    all_gather x1 -> x0, blocking collectives: 22.5 us -> none  [on_device(): ket_whole = lax.all_gather(ket_factor, 'row', axis=0, tiled=True)]
    unnamed x11 -> x5, local copies, waits for them, and re-layouts: 6.49 us -> 2.22 us
  transfers between devices with their start and end apart: 3 -> 0, of which waited for: 3 -> 0; matrix products, arithmetic and copies ran while one was open for 1% -> 0% of each run, Pallas kernels for 0% -> 0%
where the time goes in v1:
time: 84.7 us; the launch traced here: 84.4 us
  Pallas kernels  77.6 us (92%)
  local copies, waits for them, and re-layouts  4.19 us (5%)
  other arithmetic  1.95 us (2%)
    pallas_call x1, Pallas kernels, on_device(): pl.pallas_call(kernel, out_shape=(jax.ShapeDtypeStruct((3, 2, 2, KEEP, 25...  77.6 us
    unnamed x5, local copies, waits for them, and re-layouts  2.22 us

profile of v1, /device:TPU:1, one launch (start us, length us, event | category | flops | bytes accessed | tf_op | source)
XLA Modules:
  0.0 84.4 jit_solution(16018881271570399310)
XLA Ops:
  0.6 1.0 %fusion.1 = (bf16[32,2,192]{2,1,0:T(2,128)(2,1)S(1)}, bf16[32,2,192]{2,1,0:T(2,128)(2,1)S(1)}, bf16[32,2,192]{2,1,0:T(2,128)(2,1)S(1)}) fusion(bf16[32,2,512]{2,1,0:T(2,128)(2,1)} %param.4), kind=kLoop, calls=%fused_computation.7 | loop fusion | bytes 147456 | tf_op jit(solution)/shard_map/slice | solution.py:215
  1.7 0.1 stack.12
  1.8 0.1 stack.13
  1.8 0.1 stack.14
  2.0 0.9 %copy.6 = bf16[8,8,2,256]{3,1,2,0:T(8,128)(2,1)S(1)} copy(bf16[8,8,2,256]{3,2,1,0:T(2,128)(2,1)} %bitcast.13) | data formatting | bytes 131072
  2.8 0.0 copy-start
  2.8 0.7 copy-done
  3.5 0.0 copy-start.1
  3.5 0.7 copy-done.1
  4.2 77.6 %shard_map.59 = (bf16[3,2,2,176,256]{4,3,2,1,0:T(8,128)(2,1)S(1)}, f32[3,32,384]{2,1,0:T(8,128)S(1)}) custom-call(f32[2]{0:T(128)S(1)} %copy-done.1, bf16[3,32,384]{2,1,0:T(8,128)(2,1)S(1)} %pad_maximum_fusion.2.bra_ref, bf16[64,512]{1,0:T(8,128)(2,1)S(1)} %bitcast.10, f32[32,128]{1,0:T(8,128)S(1)} %bitcast.11), custom_call_target="tpu_custom_call" | custom-call | tf_op jit(solution)/shard_map/pallas_call | solution.py:218
  81.8 0.1 squeeze.22
  81.9 0.1 slice.57
  82.0 0.1 squeeze.23
  82.2 0.1 slice.58
  82.3 0.1 squeeze.21
  82.4 0.9 %pad_maximum_fusion.1 = f32[32,2,512]{2,1,0:T(2,128)} fusion(f32[32,2,176]{2,1,0:T(2,128)S(1)} %slice.58, f32[32,2,160]{2,1,0:T(2,128)S(1)} %slice.57, f32[32,2,176]{2,1,0:T(2,128)S(1)} %bitcast.12), kind=kLoop, calls=%fused_computation.4 | loop fusion | flops 65536 | bytes 262144 | tf_op jit(solution)/shard_map/concatenate | solution.py:250
  83.3 0.1 slice_bitcast_fusion.2
  83.4 1.0 %pad_maximum_fusion = bf16[2,2,512,256]{3,2,1,0:T(8,128)(2,1)} fusion(bf16[2,2,176,256]{3,2,1,0:T(8,128)(2,1)S(1)} %get-tuple-element.7, bf16[2,2,160,256]{3,2,1,0:T(8,128)(2,1)S(1)} %slice.55, bf16[2,2,176,256]{3,2,1,0:T(8,128)(2,1)S(1)} %get-tuple-element.6), kind=kLoop, calls=%fused_computation | loop fusion | flops 3145728 | bytes 2097152 | tf_op jit(solution)/shard_map/concatenate | solution.py:248
  (3 shorter events, 0.1 us)
Async XLA Ops:
  2.8 0.7 copy-start
  3.5 0.7 copy-start.1

commit v2 on v1

v2 whole, which is shorter than its diff:
```python
import functools

import jax
import jax.numpy as jnp
from jax import lax
from jax.experimental import pallas as pl
from jax.experimental.pallas import tpu as pltpu
from jax.sharding import PartitionSpec as P

NZL, NC, NY, NX, NZH = 3, 2, 8, 4, 4
WIN = 192
STARTS = (0, 160, 320)
KEEP = 176
ROWS = ((0, 176, 0), (16, 160, 176), (16, 176, 336))
BF, F32 = jnp.bfloat16, jnp.float32
NT = (((1,), (1,)), ((), ()))
TN = (((0,), (0,)), ((), ()))


def rem(value, n):
    return lax.rem(value, n)


def kernel(
    occ_ref, bra_in, ket_in, virt_ref, amp_out, gam_out,
    occ_sm, virt_vm, bra_raw, ket_raw, bra_ref, ket_ref, amp_ref, gam_ref, bra_all, ket_all, part, other, amps, va_col,
    rx_send, rx_recv, rx_own, rz_own, rz_send, rz_recv, windows,
    in_sem, own_sem, got_sem, gam_sem, bz_s, bz_r, bx_s, bx_r, kz_s, kz_r, ky_s, ky_r, p_s, p_r,
    ag_s, ag_r, fw_s, fw_r, rx_s, rx_r, rz_s, rz_r,
):
    occ, y, col = lax.axis_index("occ"), lax.axis_index("row"), lax.axis_index("col")
    zl, core = occ // 2, rem(occ, 2)
    x, zh = col // 4, rem(col, 4)

    def device(dx=0, dy=0, dzh=0, dzl=0, dcore=0):
        zl2, core2 = rem(zl + dzl, NZL), rem(core + dcore, NC)
        y2, x2, zh2 = rem(y + dy, NY), rem(x + dx, NX), rem(zh + dzh, NZH)
        return (zl2 * 2 + core2, y2, x2 * 4 + zh2)

    def send(src, dst, s_sem, r_sem, **where):
        return pltpu.make_async_remote_copy(
            src_ref=src, dst_ref=dst, send_sem=s_sem, recv_sem=r_sem,
            device_id=device(**where), device_id_type=pl.DeviceIdType.MESH,
        )

    def bra_rows(zl_src, x_src, zh_src=0):
        return pl.multiple_of(zl_src * 512 + x_src * 128 + zh_src * 32, 32)

    def ket_rows(zl_src, y_src):
        return pl.multiple_of(zl_src * 512 + y_src * 64, 64)

    z_peers = [(e, d) for e in range(3) for d in range(4) if (e, d) != (0, 0)]
    peers = [dict(dzl=e, dzh=d) for e, d in z_peers]
    peers += [dict(dx=d) for d in (1, 2, 3)] + [dict(dy=1), dict(dy=NY - 1), dict(dcore=1)]
    barrier = pltpu.get_barrier_semaphore()
    for peer in peers:
        pl.semaphore_signal(barrier, inc=1, device_id=device(**peer), device_id_type=pl.DeviceIdType.MESH)
    loads = [
        pltpu.make_async_copy(src, dst, in_sem.at[k])
        for k, (src, dst) in enumerate(
            [(bra_in, bra_raw), (ket_in, ket_raw), (virt_ref, virt_vm), (occ_ref, occ_sm)]
        )
    ]
    for load in loads:
        load.start()
    own_ket = ket_rows(zl, y)
    loads[1].wait()
    ket_wide = ket_raw[...].astype(F32)
    ket_ref[...] = jnp.concatenate([ket_wide[:, 0, :], ket_wide[:, 1, :]], axis=1).astype(BF)
    ket_all[pl.ds(own_ket, 64), :] = ket_ref[...]
    loads[0].wait()
    bra_wide = bra_raw[...].astype(F32)
    lane = lax.broadcasted_iota(jnp.int32, (32, 2 * WIN), 1)
    for w in range(3):
        part0 = pltpu.roll(bra_wide[:, 0, :], (512 - STARTS[w]) % 512, 1)[:, : 2 * WIN]
        part1 = pltpu.roll(bra_wide[:, 1, :], (512 + WIN - STARTS[w]) % 512, 1)[:, : 2 * WIN]
        bra_ref[w] = jnp.where(lane < WIN, part0, part1).astype(BF)
    bra_all[pl.ds(bra_rows(zl, x, zh), 32), :] = bra_ref[zl]
    pl.semaphore_wait(barrier, len(peers))

    pending = []

    def start(copy):
        copy.start()
        pending.append(copy)

    def ket_z(e):
        return send(ket_ref, ket_all.at[pl.ds(own_ket, 64)], kz_s.at[e], kz_r.at[e], dzl=e)

    def ket_y(e, way, step):
        zl_src = rem(zl + 3 - e, 3)
        hop = 1 if way == 0 else NY - 1
        y_src = rem(y + (NY - step + 1 if way == 0 else step - 1), NY)
        rows = ket_rows(zl_src, y_src)
        size = 64 if step < 4 else 32
        rows = pl.multiple_of(rows + (32 if step == 4 and way == 1 else 0), 32)
        here = ket_all.at[pl.ds(rows, size)]
        src = ket_ref if (step == 1 and e == 0) else here
        k = (e * 2 + way) * 4 + step - 1
        return send(src, here, ky_s.at[k], ky_r.at[k], dy=hop)

    def bra_z(e, d):
        there = bra_all.at[pl.ds(bra_rows(zl, x, zh), 32)]
        return send(bra_ref.at[rem(zl + e, 3)], there, bz_s.at[e * 4 + d], bz_r.at[e * 4 + d], dzl=e, dzh=d)

    def bra_x(e, d, dx):
        here = bra_all.at[pl.ds(bra_rows(rem(zl + 3 - e, 3), x, rem(zh + 4 - d, 4)), 32)]
        k = (e * 4 + d) * 3 + dx - 1
        src = bra_ref.at[zl] if (e, d) == (0, 0) else here
        return send(src, here, bx_s.at[k], bx_r.at[k], dx=dx)

    def ket_on(e, step):
        for way in (0, 1):
            ket_y(e, way, step).wait_recv()
            start(ket_y(e, way, step + 1))

    def bra_on(e, d):
        bra_z(e, d).wait_recv()
        for dx in (2, 1, 3):
            start(bra_x(e, d, dx))

    for e in (1, 2):
        start(ket_z(e))
    for way in (0, 1):
        start(ket_y(0, way, 1))
    for dx in (2, 1, 3):
        start(bra_x(0, 0, dx))
    near = sorted(z_peers, key=lambda p: min((p[0] + 3 * p[1]) % 12, -(p[0] + 3 * p[1]) % 12))
    for e, d in near[:7]:
        start(bra_z(e, d))

    loads[2].wait()
    loads[3].wait()
    for t in range(4):
        row = virt_vm[pl.ds(y * 4 + t, 1), :]
        va_col[pl.ds(t * 128, 128), :] = jnp.transpose(jnp.broadcast_to(row, (128, 128)))

    ket_on(0, 1)
    for e in (1, 2):
        ket_z(e).wait_recv()
        for way in (0, 1):
            start(ket_y(e, way, 1))
    steps = [(0, 2), (1, 1), (2, 1), (0, 3), (1, 2), (2, 2), (1, 3), (2, 3)]
    for k in range(3):
        ket_on(*steps[k])
    for n, piece in enumerate(near):
        bra_on(*piece)
        if n + 7 < len(near):
            start(bra_z(*near[n + 7]))
        if n % 2 == 1:
            ket_on(*steps[3 + n // 2])

    for n, e in enumerate((1, 0, 2)):
        for d in range(4):
            for dx in (1, 2, 3):
                bra_x(e, d, dx).wait_recv()
        for way in (0, 1):
            ket_y(e, way, 4).wait_recv()
        rows = pl.ds(pl.multiple_of(rem(zl + 3 - e, 3) * 512, 512), 512)
        term = lax.dot_general(bra_all[rows, :], ket_all[rows, :], TN, preferred_element_type=F32)
        if n == 0:
            part[...] = term
        else:
            part[...] += term
    swap = send(part, other, p_s.at[0], p_r.at[0], dcore=1)
    start(swap)
    vb_rows = virt_vm[pl.ds(col * 2, 2), :]
    vb = jnp.concatenate([vb_rows[0:1], vb_rows[1:2]], axis=1)
    va = va_col[pl.ds(pl.multiple_of(zl * 160, 32), WIN), :]
    va = jnp.concatenate([va, va], axis=1)
    swap.wait_recv()

    def coulomb(i, j):
        rows, cols = pl.ds(i * WIN, WIN), pl.ds(j * 256, 256)
        return part[rows, cols] + other[rows, cols]

    for i in range(2):
        for j in range(2):
            den = ((occ_sm[i] + occ_sm[j]) - va) - vb
            amps[j, pl.ds(i * WIN, WIN), :] = ((2.0 * coulomb(i, j) - coulomb(j, i)) / den).astype(BF)
    skip = pl.multiple_of(jnp.where(zl == 2, WIN - KEEP, 0), 16)

    def amp_z(e):
        src = amps.at[:, pl.ds(pl.multiple_of(core * WIN + skip, 16), KEEP), :]
        return send(src, amp_ref.at[zl, core], ag_s.at[e], ag_r.at[e], dzl=e)

    def amp_core(e):
        here = amp_ref.at[rem(zl + 3 - e, 3), core]
        return send(here, here, fw_s.at[e], fw_r.at[e], dcore=1)

    def rx(e, dx):
        k = e * 3 + dx - 1
        return send(rx_send.at[k], rx_recv.at[k], rx_s.at[k], rx_r.at[k], dx=dx)

    def rz(e, d):
        k = e * 4 + d
        return send(rz_send.at[k], rz_recv.at[k], rz_s.at[k], rz_r.at[k], dzl=e, dzh=d)

    order = (1, 2, 0)
    for n, e in enumerate(order):
        for dx in (2, 1, 3, 0):
            rows = pl.ds(bra_rows(rem(zl + e, 3), rem(x + dx, 4)), 128)
            block = lax.dot_general(ket_all[rows, 0:256], amps[0], NT, preferred_element_type=F32)
            block += lax.dot_general(ket_all[rows, 256:512], amps[1], NT, preferred_element_type=F32)
            if dx == 0:
                rx_own[e] = block
            else:
                rx_send[e * 3 + dx - 1] = block.astype(BF)
                start(rx(e, dx))
        if n == 0:
            for e2 in (1, 2):
                start(amp_z(e2))
    def own_out(w, i):
        low, size, a0 = ROWS[w]
        src = amps.at[:, pl.ds(i * WIN + low, size), :]
        return pltpu.make_async_copy(src, amp_out.at[i, :, pl.ds(a0, size), :], own_sem.at[i])

    def got_out(w, e, half):
        low, size, a0 = ROWS[w]
        i = core if half == 0 else 1 - core
        src = amp_ref.at[w, i, :, pl.ds(low if w == 1 else 0, size), :]
        return pltpu.make_async_copy(src, amp_out.at[i, :, pl.ds(a0, size), :], got_sem.at[e * 2 + half])

    def by_window(which, act):
        for w in range(3):
            pl.when(which == w)(functools.partial(act, w))

    def own_start(w):
        for i in range(2):
            own_out(w, i).start()

    def own_wait(w):
        for i in range(2):
            own_out(w, i).wait()

    by_window(zl, own_start)
    for e in order:
        for dx in (1, 2, 3):
            rx(e, dx).wait_recv()
        for d in (2, 1, 3, 0):
            rows = pl.ds(pl.multiple_of(rem(zh + d, 4) * 32, 32), 32)
            total = rx_own[e, rows, :]
            for dx in (1, 2, 3):
                total += rx_recv[e * 3 + dx - 1, rows, :].astype(F32)
            if (e, d) == (0, 0):
                rz_own[...] = total
            else:
                rz_send[e * 4 + d] = total.astype(BF)
                start(rz(e, d))
    for e in (1, 2):
        amp_z(e).wait_recv()
        start(amp_core(e))
        by_window(rem(zl + 3 - e, 3), lambda w, e=e: got_out(w, e, 0).start())
    for e in order:
        for d in range(4):
            if (e, d) != (0, 0):
                rz(e, d).wait_recv()
        total = rz_own[...] if e == 0 else rz_recv[e * 4].astype(F32)
        for d in (1, 2, 3):
            total += rz_recv[e * 4 + d].astype(F32)
        windows[rem(zl + 3 - e, 3)] = total
    for e in (1, 2):
        amp_core(e).wait_recv()
        by_window(rem(zl + 3 - e, 3), lambda w, e=e: got_out(w, e, 1).start())
    lane = lax.broadcasted_iota(jnp.int32, (32, 512), 1)
    blank = jnp.zeros((32, 128), F32)
    wide = [jnp.concatenate([windows[w], blank], axis=1) for w in range(3)]
    for i in range(2):
        turn = [pltpu.roll(wide[w], (STARTS[w] - i * WIN) % 512, 1) for w in range(3)]
        gam_ref[:, i, :] = jnp.where(lane < 176, turn[0], jnp.where(lane < 336, turn[1], turn[2]))
    gamma_copy = pltpu.make_async_copy(gam_ref, gam_out, gam_sem)
    gamma_copy.start()
    by_window(zl, own_wait)
    for e in (1, 2):
        for half in range(2):
            by_window(rem(zl + 3 - e, 3), lambda w, e=e, half=half: got_out(w, e, half).wait())
    for copy in pending:
        copy.wait_send()
    gamma_copy.wait()


def on_device(bra_factor, ket_factor, occ_energy, virt_energy):
    dma = pltpu.SemaphoreType.DMA
    hbm = pl.BlockSpec(memory_space=pl.ANY)
    return pl.pallas_call(
        kernel,
        out_shape=(
            jax.ShapeDtypeStruct((2, 2, 512, 256), BF),
            jax.ShapeDtypeStruct((32, 2, 512), F32),
        ),
        in_specs=[hbm] * 4,
        out_specs=(hbm, hbm),
        scratch_shapes=[
            pltpu.SMEM((2,), F32),
            pltpu.VMEM((32, 128), F32),
            pltpu.VMEM((32, 2, 512), BF),
            pltpu.VMEM((64, 2, 256), BF),
            pltpu.VMEM((3, 32, 2 * WIN), BF),
            pltpu.VMEM((64, 512), BF),
            pltpu.VMEM((3, 2, 2, KEEP, 256), BF),
            pltpu.VMEM((32, 2, 512), F32),
            pltpu.VMEM((1536, 2 * WIN), BF),
            pltpu.VMEM((1536, 512), BF),
            pltpu.VMEM((2 * WIN, 512), F32),
            pltpu.VMEM((2 * WIN, 512), F32),
            pltpu.VMEM((2, 2 * WIN, 256), BF),
            pltpu.VMEM((512, 128), F32),
            pltpu.VMEM((9, 128, 2 * WIN), BF),
            pltpu.VMEM((9, 128, 2 * WIN), BF),
            pltpu.VMEM((3, 128, 2 * WIN), F32),
            pltpu.VMEM((32, 2 * WIN), F32),
            pltpu.VMEM((12, 32, 2 * WIN), BF),
            pltpu.VMEM((12, 32, 2 * WIN), BF),
            pltpu.VMEM((3, 32, 2 * WIN), F32),
            dma((4,)), dma((2,)), dma((6,)), dma, dma((12,)), dma((12,)), dma((36,)), dma((36,)), dma((3,)), dma((3,)),
            dma((24,)), dma((24,)), dma((1,)), dma((1,)),
            dma((3,)), dma((3,)), dma((3,)), dma((3,)), dma((9,)), dma((9,)), dma((12,)), dma((12,)),
        ],
        compiler_params=pltpu.CompilerParams(collective_id=0, has_side_effects=True),
    )(occ_energy, bra_factor, ket_factor, virt_energy.reshape(32, 128))


def solution(mesh):
    placed = (P(("occ", "col"), None, "row"), P(("occ", "row"), None, "col"), P(), P())
    return jax.shard_map(
        on_device,
        mesh=mesh,
        in_specs=placed,
        out_specs=(P(None, None, "row", "col"), P(("occ", "col"), None, "row")),
        check_vma=False,
    )
```

time: 84.7 us -> 73.1 us (0.86)
  Pallas kernels: 77.6 us -> 69.3 us
  other arithmetic: 1.95 us -> 0 us
  local copies, waits for them, and re-layouts: 4.19 us -> 2.96 us
    pallas_call x1, Pallas kernels: 77.6 us -> 69.3 us  [on_device(): pl.pallas_call(kernel, out_shape=(jax.ShapeDtypeStruct((2, 2, 512, 256),...]
    concatenate x2 -> x0, other arithmetic: 1.93 us -> none  [the longest x1 1.04 us: on_device(): amplitudes = jnp.concatenate([amp[0], amp[1][:, :, 16:], amp[2]], axis=2)]
    slice x5 -> x0, local copies, waits for them, and re-layouts: 1.31 us -> none  [the longest x1 1.03 us: on_device(): windows = jnp.stack([bra_factor[:, :, s:s + WIN] for s in STARTS])]
    unnamed x5 -> x4, local copies, waits for them, and re-layouts: 2.22 us -> 2.96 us
where the time goes in v2:
time: 73.1 us; the launch traced here: 72.9 us
  Pallas kernels  69.3 us (95%)
  local copies, waits for them, and re-layouts  2.96 us (4%)
    pallas_call x1, Pallas kernels, on_device(): pl.pallas_call(kernel, out_shape=(jax.ShapeDtypeStruct((2, 2, 512, 256),...  69.3 us
    unnamed x4, local copies, waits for them, and re-layouts  2.96 us

profile of v2, /device:TPU:1, one launch (start us, length us, event | category | flops | bytes accessed | tf_op | source)
XLA Modules:
  0.0 72.9 jit_solution(3071319155845965797)
XLA Ops:
  0.6 69.3 %shard_map.59 = (bf16[2,2,512,256]{3,2,1,0:T(8,128)(2,1)}, f32[32,2,512]{2,1,0:T(2,128)}) custom-call(f32[2]{0:T(128)} %occ_ref.1, bf16[32,2,512]{2,1,0:T(2,128)(2,1)} %bra_in.1, bf16[64,2,256]{2,1,0:T(2,128)(2,1)} %ket_in.1, f32[32,128]{1,0:T(8,128)} %bitcast.1), custom_call_target="tpu_custom_call" | custom-call | tf_op jit(solution)/shard_map/pallas_call | solution.py:285
  70.0 0.0 copy-start
  70.0 2.3 %copy.8 = bf16[2,2,512,256]{3,2,1,0:T(8,128)(2,1)} copy(bf16[2,2,512,256]{3,2,1,0:T(8,128)(2,1)} %get-tuple-element.4) | data formatting | bytes 2097152
  72.3 0.0 copy-done
  72.3 0.7 copy.9
Async XLA Ops:
  70.0 2.3 %copy-start = (f32[32,2,512]{2,1,0:T(2,128)S(1)}, f32[32,2,512]{2,1,0:T(2,128)}, u32[]{:S(2)}) copy-start(f32[32,2,512]{2,1,0:T(2,128)} %get-tuple-element.5) | copy-start | bytes 393220

commit v3 on v2

--- a/solution.py
+++ b/solution.py
@@ -52,9 +52,6 @@
     z_peers = [(e, d) for e in range(3) for d in range(4) if (e, d) != (0, 0)]
     peers = [dict(dzl=e, dzh=d) for e, d in z_peers]
     peers += [dict(dx=d) for d in (1, 2, 3)] + [dict(dy=1), dict(dy=NY - 1), dict(dcore=1)]
-    barrier = pltpu.get_barrier_semaphore()
-    for peer in peers:
-        pl.semaphore_signal(barrier, inc=1, device_id=device(**peer), device_id_type=pl.DeviceIdType.MESH)
     loads = [
         pltpu.make_async_copy(src, dst, in_sem.at[k])
         for k, (src, dst) in enumerate(
@@ -63,19 +60,14 @@
     ]
     for load in loads:
         load.start()
+    barrier = pltpu.get_barrier_semaphore()
+    for peer in peers:
+        pl.semaphore_signal(barrier, inc=1, device_id=device(**peer), device_id_type=pl.DeviceIdType.MESH)
     own_ket = ket_rows(zl, y)
     loads[1].wait()
     ket_wide = ket_raw[...].astype(F32)
     ket_ref[...] = jnp.concatenate([ket_wide[:, 0, :], ket_wide[:, 1, :]], axis=1).astype(BF)
     ket_all[pl.ds(own_ket, 64), :] = ket_ref[...]
-    loads[0].wait()
-    bra_wide = bra_raw[...].astype(F32)
-    lane = lax.broadcasted_iota(jnp.int32, (32, 2 * WIN), 1)
-    for w in range(3):
-        part0 = pltpu.roll(bra_wide[:, 0, :], (512 - STARTS[w]) % 512, 1)[:, : 2 * WIN]
-        part1 = pltpu.roll(bra_wide[:, 1, :], (512 + WIN - STARTS[w]) % 512, 1)[:, : 2 * WIN]
-        bra_ref[w] = jnp.where(lane < WIN, part0, part1).astype(BF)
-    bra_all[pl.ds(bra_rows(zl, x, zh), 32), :] = bra_ref[zl]
     pl.semaphore_wait(barrier, len(peers))
 
     pending = []
@@ -123,17 +115,19 @@
         start(ket_z(e))
     for way in (0, 1):
         start(ket_y(0, way, 1))
+    near = sorted(z_peers, key=lambda p: min((p[0] + 3 * p[1]) % 12, -(p[0] + 3 * p[1]) % 12))
+    loads[0].wait()
+    bra_wide = bra_raw[...].astype(F32)
+    lane = lax.broadcasted_iota(jnp.int32, (32, 2 * WIN), 1)
+    for w in range(3):
+        part0 = pltpu.roll(bra_wide[:, 0, :], (512 - STARTS[w]) % 512, 1)[:, : 2 * WIN]
+        part1 = pltpu.roll(bra_wide[:, 1, :], (512 + WIN - STARTS[w]) % 512, 1)[:, : 2 * WIN]
+        bra_ref[w] = jnp.where(lane < WIN, part0, part1).astype(BF)
+    bra_all[pl.ds(bra_rows(zl, x, zh), 32), :] = bra_ref[zl]
+    for e, d in near[:7]:
+        start(bra_z(e, d))
     for dx in (2, 1, 3):
         start(bra_x(0, 0, dx))
-    near = sorted(z_peers, key=lambda p: min((p[0] + 3 * p[1]) % 12, -(p[0] + 3 * p[1]) % 12))
-    for e, d in near[:7]:
-        start(bra_z(e, d))
-
-    loads[2].wait()
-    loads[3].wait()
-    for t in range(4):
-        row = virt_vm[pl.ds(y * 4 + t, 1), :]
-        va_col[pl.ds(t * 128, 128), :] = jnp.transpose(jnp.broadcast_to(row, (128, 128)))
 
     ket_on(0, 1)
     for e in (1, 2):
@@ -149,6 +143,12 @@
             start(bra_z(*near[n + 7]))
         if n % 2 == 1:
             ket_on(*steps[3 + n // 2])
+
+    loads[2].wait()
+    loads[3].wait()
+    for t in range(4):
+        row = virt_vm[pl.ds(y * 4 + t, 1), :]
+        va_col[pl.ds(t * 128, 128), :] = jnp.transpose(jnp.broadcast_to(row, (128, 128)))
 
     for n, e in enumerate((1, 0, 2)):
         for d in range(4):

time: 73.1 us -> 72.6 us (level)
  Pallas kernels: 69.3 us -> 68.3 us
    pallas_call x1, Pallas kernels: 69.3 us -> 68.3 us  [on_device(): pl.pallas_call(kernel, out_shape=(jax.ShapeDtypeStruct((2, 2, 512, 256),...]
where the time goes in v3:
time: 72.6 us; the launch traced here: 71.9 us
  Pallas kernels  68.3 us (94%)
  local copies, waits for them, and re-layouts  2.96 us (4%)
    pallas_call x1, Pallas kernels, on_device(): pl.pallas_call(kernel, out_shape=(jax.ShapeDtypeStruct((2, 2, 512, 256),...  68.3 us
    unnamed x4, local copies, waits for them, and re-layouts  2.96 us

profile of v3, /device:TPU:1, one launch (start us, length us, event | category | flops | bytes accessed | tf_op | source)
XLA Modules:
  0.0 71.9 jit_solution(3442317953012872444)
XLA Ops:
  0.6 68.3 %shard_map.59 = (bf16[2,2,512,256]{3,2,1,0:T(8,128)(2,1)}, f32[32,2,512]{2,1,0:T(2,128)}) custom-call(f32[2]{0:T(128)} %occ_ref.1, bf16[32,2,512]{2,1,0:T(2,128)(2,1)} %bra_in.1, bf16[64,2,256]{2,1,0:T(2,128)(2,1)} %ket_in.1, f32[32,128]{1,0:T(8,128)} %bitcast.1), custom_call_target="tpu_custom_call" | custom-call | tf_op jit(solution)/shard_map/pallas_call | solution.py:285
  69.0 0.0 copy-start
  69.0 2.3 %copy.8 = bf16[2,2,512,256]{3,2,1,0:T(8,128)(2,1)} copy(bf16[2,2,512,256]{3,2,1,0:T(8,128)(2,1)} %get-tuple-element.4) | data formatting | bytes 2097152
  71.3 0.0 copy-done
  71.3 0.7 copy.9
Async XLA Ops:
  69.0 2.3 %copy-start = (f32[32,2,512]{2,1,0:T(2,128)S(1)}, f32[32,2,512]{2,1,0:T(2,128)}, u32[]{:S(2)}) copy-start(f32[32,2,512]{2,1,0:T(2,128)} %get-tuple-element.5) | copy-start | bytes 393220

commit v4 on v3

--- a/solution.py
+++ b/solution.py
@@ -108,7 +108,7 @@
 
     def bra_on(e, d):
         bra_z(e, d).wait_recv()
-        for dx in (2, 1, 3):
+        for dx in (1, 3, 2):
             start(bra_x(e, d, dx))
 
     for e in (1, 2):
@@ -126,7 +126,7 @@
     bra_all[pl.ds(bra_rows(zl, x, zh), 32), :] = bra_ref[zl]
     for e, d in near[:7]:
         start(bra_z(e, d))
-    for dx in (2, 1, 3):
+    for dx in (1, 3, 2):
         start(bra_x(0, 0, dx))
 
     ket_on(0, 1)

time: 72.6 us -> 72.1 us (level)
  no operation moved by 1% of the time
where the time goes in v4:
time: 72.1 us; the launch traced here: 71.9 us
  Pallas kernels  68.3 us (95%)
  local copies, waits for them, and re-layouts  2.96 us (4%)
    pallas_call x1, Pallas kernels, on_device(): pl.pallas_call(kernel, out_shape=(jax.ShapeDtypeStruct((2, 2, 512, 256),...  68.3 us
    unnamed x4, local copies, waits for them, and re-layouts  2.96 us

profile of v4, /device:TPU:1, one launch (start us, length us, event | category | flops | bytes accessed | tf_op | source)
XLA Modules:
  0.0 71.9 jit_solution(11401242746102699631)
XLA Ops:
  0.6 68.3 %shard_map.59 = (bf16[2,2,512,256]{3,2,1,0:T(8,128)(2,1)}, f32[32,2,512]{2,1,0:T(2,128)}) custom-call(f32[2]{0:T(128)} %occ_ref.1, bf16[32,2,512]{2,1,0:T(2,128)(2,1)} %bra_in.1, bf16[64,2,256]{2,1,0:T(2,128)(2,1)} %ket_in.1, f32[32,128]{1,0:T(8,128)} %bitcast.1), custom_call_target="tpu_custom_call" | custom-call | tf_op jit(solution)/shard_map/pallas_call | solution.py:285
  69.0 0.0 copy-start
  69.0 2.3 %copy.8 = bf16[2,2,512,256]{3,2,1,0:T(8,128)(2,1)} copy(bf16[2,2,512,256]{3,2,1,0:T(8,128)(2,1)} %get-tuple-element.4) | data formatting | bytes 2097152
  71.3 0.0 copy-done
  71.3 0.7 copy.9
Async XLA Ops:
  69.0 2.3 %copy-start = (f32[32,2,512]{2,1,0:T(2,128)S(1)}, f32[32,2,512]{2,1,0:T(2,128)}, u32[]{:S(2)}) copy-start(f32[32,2,512]{2,1,0:T(2,128)} %get-tuple-element.5) | copy-start | bytes 393220
